TPU v7x, 32 devices: a whole 2x2x4 slice. The times are simulated.
32 devices in a mesh: dp: 4 (over x, core), expert: 8 (over z, y).
Axes of the slice: x: 2, y: 2, z: 4, core: 2. Of those that a mesh axis runs over, the one named last changes fastest.
Arguments:
- tokens: bfloat16 [4096, 2048], P(('dp', 'expert')), may hold values from -6 to 6
- expert_ids: int32 [4096, 4], P(('dp', 'expert')), may hold values from 0 to 15, all different within a row; in each aligned block of 128 rows (0 to 127, 128 to 255, ...) at most 48 rows name the same one
- gate_weights: float32 [4096, 4], P(('dp', 'expert')), may hold values from 0.05 to 0.6
- grad_out: bfloat16 [4096, 2048], P(('dp', 'expert')), may hold values from -6 to 6
- w_gate: bfloat16 [16, 2048, 384], P('expert'), may hold values from -0.125 to 0.125
- w_up: bfloat16 [16, 2048, 384], P('expert'), may hold values from -0.125 to 0.125
- w_down: bfloat16 [16, 384, 2048], P('expert'), may hold values from -0.3125 to 0.3125
Outputs:
- mixed_out: bfloat16 [4096, 2048], P(('dp', 'expert'))
- d_tokens: bfloat16 [4096, 2048], P(('dp', 'expert'))
- d_gates: float32 [4096, 4], P(('dp', 'expert'))
- d_w_gate: bfloat16 [16, 2048, 384], P('expert', 'dp')
- d_w_up: bfloat16 [16, 2048, 384], P('expert', 'dp')
- d_w_down: bfloat16 [16, 384, 2048], P('expert', None, 'dp')
Inputs may be any that keep to these rules, and one draw needn't show every extreme that they name: `expert_ids`: each row names 4 different experts; in the 128 rows of one device no expert is named more than 48 times, and in every draw some expert is named exactly 48 times by the rows of some device.
All inputs are finite; a program needn't handle non-finite values.
Results may differ from a plain program's by a relative error of at most 0.009.
Values may be sent and summed in bfloat16 or wider, within the bound.
A program may use at most 128 MiB of HBM per device.

v0:
```python
import jax
import jax.numpy as jnp
from jax import lax
from jax.sharding import PartitionSpec as P

BF16 = jnp.bfloat16
F32 = jnp.float32


def dot(spec, a, b):
    return jnp.einsum(spec, a, b, preferred_element_type=F32)


def local(tokens, expert_ids, gate_weights, grad_out, w_gate, w_up, w_down):
    tok_dev, model_dim = tokens.shape
    exp_dev = w_gate.shape[0]
    owners = lax.axis_size("expert")
    experts = exp_dev * owners
    me = lax.axis_index("expert")
    chosen = expert_ids[:, :, None] == jnp.arange(experts, dtype=jnp.int32)
    gate_of = jnp.sum(jnp.where(chosen, gate_weights[:, :, None], 0.0), axis=1)
    gates = lax.all_to_all(
        gate_of.reshape(tok_dev, owners, exp_dev).transpose(1, 2, 0), "expert", 0, 0, tiled=True
    )
    gates = gates.transpose(1, 0, 2).reshape(exp_dev, owners * tok_dev, 1)
    rows = lax.all_gather(tokens, "expert", axis=0, tiled=True)
    grads = lax.all_gather(grad_out, "expert", axis=0, tiled=True)
    gate_pre = dot("td,edf->etf", rows, w_gate)
    up_pre = dot("td,edf->etf", rows, w_up)
    d_mid = dot("td,efd->etf", grads, w_down)
    sigma = jax.nn.sigmoid(gate_pre)
    hidden = gate_pre * sigma * up_pre
    d_gate_sum = jnp.sum(hidden * d_mid, axis=2)
    d_hidden = gates * d_mid
    scaled_hidden = (gates * hidden).astype(BF16)
    d_up = (d_hidden * gate_pre * sigma).astype(BF16)
    d_gate = (d_hidden * up_pre * sigma * (1.0 + gate_pre * (1.0 - sigma))).astype(BF16)
    mixed = dot("etf,efd->td", scaled_hidden, w_down).astype(BF16)
    mixed_out = lax.psum_scatter(mixed, "expert", scatter_dimension=0, tiled=True)
    d_rows = (dot("etf,edf->td", d_gate, w_gate) + dot("etf,edf->td", d_up, w_up)).astype(BF16)
    d_tokens = lax.psum_scatter(d_rows, "expert", scatter_dimension=0, tiled=True)
    back = lax.all_to_all(
        d_gate_sum.reshape(exp_dev, owners, tok_dev).transpose(1, 0, 2), "expert", 0, 0, tiled=True
    )
    back = back.reshape(experts, tok_dev).T
    d_gates = jnp.sum(jnp.where(chosen, back[:, None, :], 0.0), axis=2)
    part_gate = dot("td,etf->edf", rows, d_gate).astype(BF16)
    part_up = dot("td,etf->edf", rows, d_up).astype(BF16)
    part_down = dot("etf,td->efd", scaled_hidden, grads).astype(BF16)
    grad_gate = lax.psum_scatter(part_gate, "dp", scatter_dimension=1, tiled=True)
    grad_up = lax.psum_scatter(part_up, "dp", scatter_dimension=1, tiled=True)
    grad_down = lax.psum_scatter(part_down, "dp", scatter_dimension=2, tiled=True)
    return (mixed_out, d_tokens, d_gates, grad_gate, grad_up, grad_down)


def solution(mesh):
    in_specs = (
        P(("dp", "expert"), None),
        P(("dp", "expert"), None),
        P(("dp", "expert"), None),
        P(("dp", "expert"), None),
        P("expert", None, None),
        P("expert", None, None),
        P("expert", None, None),
    )
    out_specs = (
        P(("dp", "expert"), None),
        P(("dp", "expert"), None),
        P(("dp", "expert"), None),
        P("expert", "dp", None),
        P("expert", "dp", None),
        P("expert", None, "dp"),
    )
    return jax.shard_map(local, mesh=mesh, in_specs=in_specs, out_specs=out_specs, check_vma=False)
```

profile of v0, /device:TPU:0, one launch (start us, length us, event | category | flops | bytes accessed | tf_op | source)
XLA Modules:
  0.0 501.6 jit_solution(12466991907737185224)
XLA Ops:
  7.2 0.0 all-gather.3.cloned.1.call-start
  7.2 0.7 all-gather.3.cloned.1.call-update
  7.9 0.0 all-gather.5.cloned.1.call-start
  8.0 0.7 all-gather.5.cloned.1.call-update
  8.7 0.0 reduce-scatter.10.cloned.1.call-start
  8.7 77.0 %all-gather.3.cloned.1.call-done = bf16[1024,2048]{1,0:T(8,128)(2,1)} async-done(((bf16[128,2048]{1,0:T(8,128)(2,1)}), bf16[1024,2048]{1,0:T(8,128)(2,1)}) %all-gather.3.cloned.1.call-update) | async-done | bytes 4194320 | tf_op jit(solution)/shard_map/all_gather | solution.py:26
  85.7 8.4 %fusion.9 = f32[2,384,1024]{2,1,0:T(8,128)} fusion(bf16[2,2048,384]{2,1,0:T(8,128)(2,1)} %param.12, bf16[1024,2048]{1,0:T(8,128)(2,1)} %all-gather.3.cloned.1.call-done), kind=kOutput, calls=%fused_computation.11 | convolution fusion | flops 3221225472 | bytes 10485760 | tf_op jit(solution)/shard_map/td,edf->etf/dot_general | solution.py:11
  94.0 5.1 %fusion.11 = f32[2,384,1024]{2,1,0:T(8,128)} fusion(bf16[2,2048,384]{2,1,0:T(8,128)(2,1)S(1)} %copy-done.9, bf16[1024,2048]{1,0:T(8,128)(2,1)S(1)} %copy-done.7), kind=kOutput, calls=%fused_computation.13 | convolution fusion | flops 3221225472 | bytes 10485760 | tf_op jit(solution)/shard_map/td,edf->etf/dot_general | solution.py:11
  99.1 60.0 %all-gather.5.cloned.1.call-done = bf16[1024,2048]{1,0:T(8,128)(2,1)} async-done(((bf16[128,2048]{1,0:T(8,128)(2,1)}), bf16[1024,2048]{1,0:T(8,128)(2,1)}) %all-gather.5.cloned.1.call-update) | async-done | bytes 4194320 | tf_op jit(solution)/shard_map/all_gather | solution.py:27
  159.2 7.3 %fusion.22 = (f32[2,1024]{1,0:T(2,128)S(1)}, f32[2,384,1024]{2,1,0:T(8,128)S(1)}) fusion(f32[2,384,1024]{2,1,0:T(8,128)} %fusion.9, f32[2,384,1024]{2,1,0:T(8,128)} %fusion.11, bf16[2,384,2048]{2,1,0:T(8,128)(2,1)S(1)} %copy-done, bf16[1024,2048]{1,0:T(8,128)(2,1)} %all-gather.5.cloned.1.call-done), kind=kOutput, calls=%fused_computation.20 | convolution fusion | flops 3226728448 | bytes 16785408 | tf_op jit(solution)/shard_map/td,efd->etf/dot_general | solution.py:11
  166.5 9.5 %all_to_all.10 = f32[8,2,128]{2,1,0:T(2,128)S(1)} all-to-all(f32[8,2,128]{2,1,0:T(2,128)S(1)} %copy.49), channel_id=1, replica_groups=mesh['dp'=4,'expert'=8] {'expert'}, dimensions={0} | all-to-all | bytes 16384 | tf_op jit(solution)/shard_map/all_to_all | solution.py:42
  175.9 0.6 select_reduce_fusion
  176.5 8.9 %all_to_all.11 = f32[8,2,128]{2,1,0:T(2,128)S(1)} all-to-all(f32[8,2,128]{2,1,0:T(2,128)S(1)} %bitcast.127), channel_id=1, replica_groups=mesh['dp'=4,'expert'=8] {'expert'}, dimensions={0} | all-to-all | bytes 16384 | tf_op jit(solution)/shard_map/all_to_all | solution.py:22
  185.4 2.8 fusion.31
  188.2 1.2 copy-done.4
  189.4 4.8 fusion.35
  194.2 0.0 reduce-scatter.12.cloned.1.call-start
  194.3 7.8 %fusion.32 = bf16[2,2048,384]{1,2,0:T(8,128)(2,1)} fusion(bf16[2,1024,384]{1,2,0:T(8,128)(2,1)} %get-tuple-element.32, bf16[1024,2048]{1,0:T(8,128)(2,1)} %all-gather.3.cloned.1.call-done), kind=kOutput, calls=%fused_computation.37 | convolution fusion | flops 3222798336 | bytes 8912896 | tf_op jit(solution)/shard_map/td,etf->edf/dot_general | solution.py:11
  202.1 0.0 reduce-scatter.14.cloned.1.call-start
  202.2 9.2 %fusion.19 = bf16[2,384,2048]{2,1,0:T(8,128)(2,1)} fusion(bf16[1024,2048]{1,0:T(8,128)(2,1)} %all-gather.5.cloned.1.call-done, f32[2,1024]{1,0:T(2,128)S(1)} %bitcast.129, f32[2,384,1024]{2,1,0:T(8,128)} %fusion.9, f32[2,384,1024]{2,1,0:T(8,128)} %fusion.11), kind=kOutput, calls=%fused_computation.17 | convolution fusion | flops 3228303360 | bytes 13639680 | tf_op jit(solution)/shard_map/etf,td->efd/dot_general | solution.py:11
  211.4 0.0 reduce-scatter.6.cloned.1.call-start
  211.5 8.1 %bitcast_convert_fusion = bf16[1024,2048]{1,0:T(8,128)(2,1)} fusion(bf16[2,384,2048]{2,1,0:T(8,128)(2,1)S(1)} %copy-done, f32[2,1024]{1,0:T(2,128)S(1)} %bitcast.130, f32[2,384,1024]{2,1,0:T(8,128)} %fusion.9, f32[2,384,1024]{2,1,0:T(8,128)} %fusion.11), kind=kOutput, calls=%fused_computation.2 | convolution fusion | flops 3228827648 | bytes 13639680 | tf_op jit(solution)/shard_map/etf,efd->td/dot_general | solution.py:11
  219.6 0.3 reduce-scatter.8.cloned.1.call-start
  219.9 6.1 %fusion.38 = f32[1024,2048,1]{1,0,2:T(8,128)S(1)} fusion(bf16[2,1024,384]{1,2,0:T(8,128)(2,1)} %copy-done.4, bf16[2,2048,384]{2,1,0:T(8,128)(2,1)} %param.11), kind=kOutput, calls=%fused_computation.43 | convolution fusion | flops 3221225472 | bytes 13107200 | tf_op jit(solution)/shard_map/etf,edf->td/dot_general | solution.py:11
  226.0 5.1 %fusion = bf16[1024,2048]{1,0:T(8,128)(2,1)} fusion(f32[1024,2048,1]{1,0,2:T(8,128)S(1)} %fusion.38, bf16[2,1024,384]{1,2,0:T(8,128)(2,1)S(1)} %copy-done.3, bf16[2,2048,384]{2,1,0:T(8,128)(2,1)S(1)} %copy-done.10), kind=kOutput, calls=%fused_computation.1 | convolution fusion | flops 3225419776 | bytes 17301504 | tf_op jit(solution)/shard_map/etf,edf->td/dot_general | solution.py:11
  231.1 0.0 reduce-scatter.10.cloned.1.call-done
  231.2 2.3 copy.50
  233.4 36.0 %reduce-scatter.12.cloned.1.call-done = bf16[2,512,384]{1,2,0:T(8,128)(2,1)} async-done(((bf16[2,2048,384]{1,2,0:T(8,128)(2,1)}), bf16[2,512,384]{1,2,0:T(8,128)(2,1)}) %reduce-scatter.12.cloned.1.call-update) | async-done | bytes 786448 | tf_op jit(solution)/shard_map/reduce_scatter | solution.py:51
  269.5 2.3 copy.51
  271.8 38.4 %reduce-scatter.14.cloned.1.call-done = bf16[2,384,512]{2,1,0:T(8,128)(2,1)} async-done(((bf16[2,384,2048]{2,1,0:T(8,128)(2,1)}), bf16[2,384,512]{2,1,0:T(8,128)(2,1)}) %reduce-scatter.14.cloned.1.call-update) | async-done | bytes 786448 | tf_op jit(solution)/shard_map/reduce_scatter | solution.py:52
  310.2 92.4 %reduce-scatter.6.cloned.1.call-done = bf16[128,2048]{1,0:T(8,128)(2,1)} async-done(((bf16[1024,2048]{1,0:T(8,128)(2,1)}), bf16[128,2048]{1,0:T(8,128)(2,1)}) %reduce-scatter.6.cloned.1.call-update) | async-done | bytes 524304 | tf_op jit(solution)/shard_map/reduce_scatter | solution.py:39
  402.6 92.2 %reduce-scatter.8.cloned.1.call-done = bf16[128,2048]{1,0:T(8,128)(2,1)} async-done(((bf16[1024,2048]{1,0:T(8,128)(2,1)}), bf16[128,2048]{1,0:T(8,128)(2,1)}) %reduce-scatter.8.cloned.1.call-update) | async-done | bytes 524304 | tf_op jit(solution)/shard_map/reduce_scatter | solution.py:41
  (28 shorter events, 0.1 us)
Async XLA Ops:
  7.2 152.0 %copy-start = (bf16[2,384,2048]{2,1,0:T(8,128)(2,1)S(1)}, bf16[2,384,2048]{2,1,0:T(8,128)(2,1)}, u32[]{:S(2)}) copy-start(bf16[2,384,2048]{2,1,0:T(8,128)(2,1)} %param.13) | copy-start | bytes 9437188
  7.2 78.5 %all-gather.3.cloned.1.call-start = ((), (), s32[]{:S(2)}) async-start(), calls=%async_computation.7 | async-start | bytes 4718592 | tf_op jit(solution)/shard_map/all_gather | solution.py:26
  7.9 151.2 %all-gather.5.cloned.1.call-start = ((), (), s32[]{:S(2)}) async-start(), calls=%async_computation.9 | async-start | bytes 4718592 | tf_op jit(solution)/shard_map/all_gather | solution.py:27
  8.7 222.5 %reduce-scatter.10.cloned.1.call-start = ((), (), s32[]{:S(2)}) async-start(), calls=%async_computation.11 | async-start | bytes 3932160 | tf_op jit(solution)/shard_map/reduce_scatter | solution.py:50
  85.7 8.4 %copy-start.7 = (bf16[1024,2048]{1,0:T(8,128)(2,1)S(1)}, bf16[1024,2048]{1,0:T(8,128)(2,1)}, u32[]{:S(2)}) copy-start(bf16[1024,2048]{1,0:T(8,128)(2,1)} %all-gather.3.cloned.1.call-done) | copy-start | bytes 12582916
  85.7 8.4 %copy-start.9 = (bf16[2,2048,384]{2,1,0:T(8,128)(2,1)S(1)}, bf16[2,2048,384]{2,1,0:T(8,128)(2,1)}, u32[]{:S(2)}) copy-start(bf16[2,2048,384]{2,1,0:T(8,128)(2,1)} %param.11) | copy-start | bytes 9437188
  99.1 76.8 %copy-start.5 = (s32[128,4]{0,1:T(4,128)S(1)}, s32[128,4]{0,1:T(4,128)}, u32[]{:S(2)}) copy-start(s32[128,4]{0,1:T(4,128)} %param.8) | copy-start | bytes 6148
  99.1 76.8 %copy-start.6 = (f32[128,4]{0,1:T(4,128)S(1)}, f32[128,4]{0,1:T(4,128)}, u32[]{:S(2)}) copy-start(f32[128,4]{0,1:T(4,128)} %param.9) | copy-start | bytes 6148
  159.1 26.3 %copy-start.1 = (f32[2,384,1024]{2,1,0:T(8,128)S(1)}, f32[2,384,1024]{2,1,0:T(8,128)}, u32[]{:S(2)}) copy-start(f32[2,384,1024]{2,1,0:T(8,128)} %fusion.9) | copy-start | bytes 9437188
  159.1 26.3 %copy-start.2 = (f32[2,384,1024]{2,1,0:T(8,128)S(1)}, f32[2,384,1024]{2,1,0:T(8,128)}, u32[]{:S(2)}) copy-start(f32[2,384,1024]{2,1,0:T(8,128)} %fusion.11) | copy-start | bytes 9437188
  185.4 4.0 copy-start.8
  188.2 1.2 copy-start.4
  194.2 75.2 %reduce-scatter.12.cloned.1.call-start = ((), (), s32[]{:S(2)}) async-start(), calls=%async_computation.12 | async-start | bytes 3932160 | tf_op jit(solution)/shard_map/reduce_scatter | solution.py:51
  202.1 108.0 %reduce-scatter.14.cloned.1.call-start = ((), (), s32[]{:S(2)}) async-start(), calls=%async_computation.13 | async-start | bytes 3932160 | tf_op jit(solution)/shard_map/reduce_scatter | solution.py:52
  211.4 191.1 %reduce-scatter.6.cloned.1.call-start = ((), (), s32[]{:S(2)}) async-start(), calls=%async_computation.8 | async-start | bytes 4718592 | tf_op jit(solution)/shard_map/reduce_scatter | solution.py:39
  219.6 275.2 %reduce-scatter.8.cloned.1.call-start = ((), (), s32[]{:S(2)}) async-start(), calls=%async_computation.10 | async-start | bytes 4718592 | tf_op jit(solution)/shard_map/reduce_scatter | solution.py:41
  219.9 6.1 %copy-start.3 = (bf16[2,1024,384]{1,2,0:T(8,128)(2,1)S(1)}, bf16[2,1024,384]{1,2,0:T(8,128)(2,1)}, u32[]{:S(2)}) copy-start(bf16[2,1024,384]{1,2,0:T(8,128)(2,1)} %get-tuple-element.32) | copy-start | bytes 4718596
  219.9 6.1 %copy-start.10 = (bf16[2,2048,384]{2,1,0:T(8,128)(2,1)S(1)}, bf16[2,2048,384]{2,1,0:T(8,128)(2,1)}, u32[]{:S(2)}) copy-start(bf16[2,2048,384]{2,1,0:T(8,128)(2,1)} %param.12) | copy-start | bytes 9437188
Sparse Core Ops, SparseCore 0:
  10.1 75.5 all-gather.2
  87.8 71.3 all-gather.4
  194.3 34.9 reduce-scatter.9
  231.7 37.7 reduce-scatter.11
  272.4 37.7 reduce-scatter.13
  314.2 88.3 reduce-scatter.5
  406.8 87.9 reduce-scatter.7
where the time goes:
time: 502 us
  waiting for transfers between devices  398 us (79%)
  matrix products  61.9 us (12%)
  blocking collectives  18.3 us (4%)
  between operations  14.2 us (3%)
  local copies, waits for them, and re-layouts  5.78 us (1%)
    reduce_scatter x1, waiting for transfers between devices, local(): lax.psum_scatter(mixed, 'expert', scatter_dimension=0, tiled=True)  92.4 us
    reduce_scatter x1, waiting for transfers between devices, local(): lax.psum_scatter(d_rows, 'expert', scatter_dimension=0, tiled=True)  92.2 us
    all_gather x1, waiting for transfers between devices, local(): rows = lax.all_gather(tokens, 'expert', axis=0, tiled=True)  77 us
    dot_general x9, matrix products, dot(): return jnp.einsum(spec, a, b, preferred_element_type=F32)  61.9 us
    all_gather x1, waiting for transfers between devices, local(): grads = lax.all_gather(grad_out, 'expert', axis=0, tiled=True)  60 us
    reduce_scatter x1, waiting for transfers between devices, local(): lax.psum_scatter(part_down, 'dp', scatter_dimension=2, tiled=True)  38.4 us
    reduce_scatter x1, waiting for transfers between devices, local(): grad_up = lax.psum_scatter(part_up, 'dp', scatter_dimension=1, tiled=True)  36 us
  transfers between devices with their start and end apart: 7, of which 6 were waited for; matrix products, arithmetic and copies ran while one was open for 11% of the time, Pallas kernels for 0%

commit v1 on v0

--- a/solution.py
+++ b/solution.py
@@ -23,8 +23,11 @@
         gate_of.reshape(tok_dev, owners, exp_dev).transpose(1, 2, 0), "expert", 0, 0, tiled=True
     )
     gates = gates.transpose(1, 0, 2).reshape(exp_dev, owners * tok_dev, 1)
-    rows = lax.all_gather(tokens, "expert", axis=0, tiled=True)
-    grads = lax.all_gather(grad_out, "expert", axis=0, tiled=True)
+    rows, grads = jnp.split(
+        lax.all_gather(jnp.concatenate([tokens, grad_out], axis=1), "expert", axis=0, tiled=True),
+        [tokens.shape[1]],
+        axis=1,
+    )
     gate_pre = dot("td,edf->etf", rows, w_gate)
     up_pre = dot("td,edf->etf", rows, w_up)
     d_mid = dot("td,efd->etf", grads, w_down)

time: 502 us -> 486 us (0.968)
  waiting for transfers between devices: 398 us -> 386 us
  matrix products: 61.9 us -> 55.1 us
    reduce_scatter x1, waiting for transfers between devices: 36 us -> 0.02 us  [local(): grad_up = lax.psum_scatter(part_up, 'dp', scatter_dimension=1, tiled=True)]
    reduce_scatter x1, waiting for transfers between devices: 0.02 us -> 35.9 us  [local(): lax.psum_scatter(part_gate, 'dp', scatter_dimension=1, tiled=True)]
    all_gather x2 -> x1, waiting for transfers between devices: 137 us -> 128 us  [local(): lax.all_gather(jnp.concatenate([tokens, grad_out], axis=1), 'expert', axi...]
    dot_general x9, matrix products: 61.9 us -> 55.1 us  [dot(): return jnp.einsum(spec, a, b, preferred_element_type=F32)]
  transfers between devices with their start and end apart: 7 -> 6, of which waited for: 6 -> 5; matrix products, arithmetic and copies ran while one was open for 11% -> 8% of each run, Pallas kernels for 0% -> 0%
where the time goes in v1:
time: 486 us
  waiting for transfers between devices  386 us (79%)
  matrix products  55.1 us (11%)
  blocking collectives  18 us (4%)
  between operations  14.2 us (3%)
  other arithmetic  5.89 us (1%)
  local copies, waits for them, and re-layouts  5.83 us (1%)
    all_gather x1, waiting for transfers between devices, local(): lax.all_gather(jnp.concatenate([tokens, grad_out], axis=1), 'expert', axi...  128 us
    reduce_scatter x1, waiting for transfers between devices, local(): lax.psum_scatter(mixed, 'expert', scatter_dimension=0, tiled=True)  92.4 us
    reduce_scatter x1, waiting for transfers between devices, local(): lax.psum_scatter(d_rows, 'expert', scatter_dimension=0, tiled=True)  92 us
    dot_general x9, matrix products, dot(): return jnp.einsum(spec, a, b, preferred_element_type=F32)  55.1 us
    reduce_scatter x1, waiting for transfers between devices, local(): lax.psum_scatter(part_down, 'dp', scatter_dimension=2, tiled=True)  38.5 us
    reduce_scatter x1, waiting for transfers between devices, local(): lax.psum_scatter(part_gate, 'dp', scatter_dimension=1, tiled=True)  35.9 us
  transfers between devices with their start and end apart: 6, of which 5 were waited for; matrix products, arithmetic and copies ran while one was open for 8% of the time, Pallas kernels for 0%

profile of v1, /device:TPU:0, one launch (start us, length us, event | category | flops | bytes accessed | tf_op | source)
XLA Modules:
  0.0 486.2 jit_solution(5482124329749433344)
XLA Ops:
  7.2 0.0 all-gather.2.cloned.1.call-start
  7.2 2.5 pad_maximum_fusion
  9.7 0.0 all-gather.2.cloned.1.call-update
  9.7 0.0 reduce-scatter.12.cloned.1.call-start
  9.8 127.6 %all-gather.2.cloned.1.call-done = bf16[1024,4096]{1,0:T(8,128)(2,1)} async-done(((bf16[128,4096]{1,0:T(8,128)(2,1)}), bf16[1024,4096]{1,0:T(8,128)(2,1)}) %all-gather.2.cloned.1.call-update) | async-done | bytes 8388624 | tf_op jit(solution)/shard_map/all_gather | solution.py:27
  137.4 6.4 %fusion.14 = f32[1024,2,384]{0,2,1:T(8,128)S(1)} fusion(bf16[2,2048,384]{2,1,0:T(8,128)(2,1)} %param.12, bf16[1024,4096]{1,0:T(8,128)(2,1)} %all-gather.2.cloned.1.call-done), kind=kOutput, calls=%fused_computation.30 | convolution fusion | flops 3221225472 | bytes 10485760 | tf_op jit(solution)/shard_map/td,edf->etf/dot_general | solution.py:11
  143.7 0.0 copy-done.8
  143.8 3.6 fusion.15
  147.5 3.9 fusion.2
  151.4 9.1 %all_to_all.10 = f32[8,2,128]{2,1,0:T(2,128)S(1)} all-to-all(f32[8,2,128]{2,1,0:T(2,128)S(1)} %copy.49), channel_id=1, replica_groups=mesh['dp'=4,'expert'=8] {'expert'}, dimensions={0} | all-to-all | bytes 16384 | tf_op jit(solution)/shard_map/all_to_all | solution.py:45
  160.5 0.6 select_reduce_fusion
  161.1 8.9 %all_to_all.11 = f32[8,2,128]{2,1,0:T(2,128)S(1)} all-to-all(f32[8,2,128]{2,1,0:T(2,128)S(1)} %bitcast.113), channel_id=1, replica_groups=mesh['dp'=4,'expert'=8] {'expert'}, dimensions={0} | all-to-all | bytes 16384 | tf_op jit(solution)/shard_map/all_to_all | solution.py:22
  170.0 2.8 fusion.11
  172.8 1.2 copy-done.3
  173.9 4.8 fusion.13
  178.7 0.0 reduce-scatter.12.cloned.1.call-update
  178.8 0.2 reduce-scatter.10.cloned.1.call-start
  179.0 8.0 %fusion.12 = bf16[2,2048,384]{1,2,0:T(8,128)(2,1)} fusion(bf16[2,1024,384]{1,2,0:T(8,128)(2,1)} %get-tuple-element.33, bf16[1024,4096]{1,0:T(8,128)(2,1)} %all-gather.2.cloned.1.call-done), kind=kOutput, calls=%fused_computation.28 | convolution fusion | flops 3222798336 | bytes 8912896 | tf_op jit(solution)/shard_map/td,etf->edf/dot_general | solution.py:11
  187.0 0.0 reduce-scatter.14.cloned.1.call-start
  187.0 9.2 %convolution_convert_fusion = bf16[2,384,2048]{2,1,0:T(8,128)(2,1)} fusion(bf16[1024,4096]{1,0:T(8,128)(2,1)} %all-gather.2.cloned.1.call-done, f32[2,1024]{1,0:T(2,128)S(1)} %bitcast.115, f32[1024,2,384]{0,2,1:T(8,128)} %copy-done.1, f32[1024,2,384]{0,2,1:T(8,128)} %copy-done.2), kind=kOutput, calls=%fused_computation.5 | convolution fusion | flops 3228303360 | bytes 13639680 | tf_op jit(solution)/shard_map/etf,td->efd/dot_general | solution.py:11
  196.3 0.0 reduce-scatter.6.cloned.1.call-start
  196.3 8.1 %bitcast_convert_fusion = bf16[1024,2048]{1,0:T(8,128)(2,1)} fusion(bf16[2,384,2048]{2,1,0:T(8,128)(2,1)S(1)} %copy-done, f32[2,1024]{1,0:T(2,128)S(1)} %bitcast.116, f32[1024,2,384]{0,2,1:T(8,128)} %copy-done.1, f32[1024,2,384]{0,2,1:T(8,128)} %copy-done.2), kind=kOutput, calls=%fused_computation.2 | convolution fusion | flops 3228827648 | bytes 13639680 | tf_op jit(solution)/shard_map/etf,efd->td/dot_general | solution.py:11
  204.4 0.3 reduce-scatter.8.cloned.1.call-start
  204.7 6.1 %fusion.16 = f32[1024,2048,1]{1,0,2:T(8,128)S(1)} fusion(bf16[2,1024,384]{1,2,0:T(8,128)(2,1)} %get-tuple-element.33, bf16[2,2048,384]{2,1,0:T(8,128)(2,1)} %param.11), kind=kOutput, calls=%fused_computation.37 | convolution fusion | flops 3221225472 | bytes 13107200 | tf_op jit(solution)/shard_map/etf,edf->td/dot_general | solution.py:11
  210.8 5.1 %fusion = bf16[1024,2048]{1,0:T(8,128)(2,1)} fusion(f32[1024,2048,1]{1,0,2:T(8,128)S(1)} %fusion.16, bf16[2,1024,384]{1,2,0:T(8,128)(2,1)S(1)} %copy-done.4, bf16[2,2048,384]{2,1,0:T(8,128)(2,1)S(1)} %copy-done.9), kind=kOutput, calls=%fused_computation.1 | convolution fusion | flops 3225419776 | bytes 17301504 | tf_op jit(solution)/shard_map/etf,edf->td/dot_general | solution.py:11
  215.9 0.0 reduce-scatter.12.cloned.1.call-done
  215.9 2.3 copy.51
  218.2 35.9 %reduce-scatter.10.cloned.1.call-done = bf16[2,512,384]{1,2,0:T(8,128)(2,1)} async-done(((bf16[2,2048,384]{1,2,0:T(8,128)(2,1)}), bf16[2,512,384]{1,2,0:T(8,128)(2,1)}) %reduce-scatter.10.cloned.1.call-update) | async-done | bytes 786448 | tf_op jit(solution)/shard_map/reduce_scatter | solution.py:53
  254.2 2.3 copy.50
  256.4 38.5 %reduce-scatter.14.cloned.1.call-done = bf16[2,384,512]{2,1,0:T(8,128)(2,1)} async-done(((bf16[2,384,2048]{2,1,0:T(8,128)(2,1)}), bf16[2,384,512]{2,1,0:T(8,128)(2,1)}) %reduce-scatter.14.cloned.1.call-update) | async-done | bytes 786448 | tf_op jit(solution)/shard_map/reduce_scatter | solution.py:55
  294.9 92.4 %reduce-scatter.6.cloned.1.call-done = bf16[128,2048]{1,0:T(8,128)(2,1)} async-done(((bf16[1024,2048]{1,0:T(8,128)(2,1)}), bf16[128,2048]{1,0:T(8,128)(2,1)}) %reduce-scatter.6.cloned.1.call-update) | async-done | bytes 524304 | tf_op jit(solution)/shard_map/reduce_scatter | solution.py:42
  387.3 92.0 %reduce-scatter.8.cloned.1.call-done = bf16[128,2048]{1,0:T(8,128)(2,1)} async-done(((bf16[1024,2048]{1,0:T(8,128)(2,1)}), bf16[128,2048]{1,0:T(8,128)(2,1)}) %reduce-scatter.8.cloned.1.call-update) | async-done | bytes 524304 | tf_op jit(solution)/shard_map/reduce_scatter | solution.py:44
  (24 shorter events, 0.1 us)
Async XLA Ops:
  7.2 140.3 %copy-start = (bf16[2,384,2048]{2,1,0:T(8,128)(2,1)S(1)}, bf16[2,384,2048]{2,1,0:T(8,128)(2,1)}, u32[]{:S(2)}) copy-start(bf16[2,384,2048]{2,1,0:T(8,128)(2,1)} %param.13) | copy-start | bytes 9437188
  7.2 130.2 %all-gather.2.cloned.1.call-start = ((), (), s32[]{:S(2)}) async-start(), calls=%async_computation.7 | async-start | bytes 9437184 | tf_op jit(solution)/shard_map/all_gather | solution.py:27
  9.7 206.2 %reduce-scatter.12.cloned.1.call-start = ((), (), s32[]{:S(2)}) async-start(), calls=%async_computation.11 | async-start | bytes 3932160 | tf_op jit(solution)/shard_map/reduce_scatter | solution.py:54
  137.3 6.4 %copy-start.7 = (bf16[1024,4096]{1,0:T(8,128)(2,1)S(1)}, bf16[1024,4096]{1,0:T(8,128)(2,1)}, u32[]{:S(2)}) copy-start(bf16[1024,4096]{1,0:T(8,128)(2,1)} %all-gather.2.cloned.1.call-done) | copy-start | bytes 25165828
  137.3 6.4 %copy-start.8 = (bf16[2,2048,384]{2,1,0:T(8,128)(2,1)S(1)}, bf16[2,2048,384]{2,1,0:T(8,128)(2,1)}, u32[]{:S(2)}) copy-start(bf16[2,2048,384]{2,1,0:T(8,128)(2,1)} %param.11) | copy-start | bytes 9437188
  143.8 26.2 %copy-start.1 = (f32[1024,2,384]{0,2,1:T(8,128)}, f32[1024,2,384]{0,2,1:T(8,128)S(1)}, u32[]{:S(2)}) copy-start(f32[1024,2,384]{0,2,1:T(8,128)S(1)} %fusion.14) | copy-start | bytes 9437188
  147.4 22.5 %copy-start.2 = (f32[1024,2,384]{0,2,1:T(8,128)}, f32[1024,2,384]{0,2,1:T(8,128)S(1)}, u32[]{:S(2)}) copy-start(f32[1024,2,384]{0,2,1:T(8,128)S(1)} %fusion.15) | copy-start | bytes 9437188
  147.5 13.0 %copy-start.5 = (s32[128,4]{0,1:T(4,128)S(1)}, s32[128,4]{0,1:T(4,128)}, u32[]{:S(2)}) copy-start(s32[128,4]{0,1:T(4,128)} %param.8) | copy-start | bytes 6148
  147.5 13.0 %copy-start.6 = (f32[128,4]{0,1:T(4,128)S(1)}, f32[128,4]{0,1:T(4,128)}, u32[]{:S(2)}) copy-start(f32[128,4]{0,1:T(4,128)} %param.9) | copy-start | bytes 6148
  172.8 1.2 copy-start.3
  178.8 75.4 %reduce-scatter.10.cloned.1.call-start = ((), (), s32[]{:S(2)}) async-start(), calls=%async_computation.10 | async-start | bytes 3932160 | tf_op jit(solution)/shard_map/reduce_scatter | solution.py:53
  187.0 107.9 %reduce-scatter.14.cloned.1.call-start = ((), (), s32[]{:S(2)}) async-start(), calls=%async_computation.12 | async-start | bytes 3932160 | tf_op jit(solution)/shard_map/reduce_scatter | solution.py:55
  196.3 191.0 %reduce-scatter.6.cloned.1.call-start = ((), (), s32[]{:S(2)}) async-start(), calls=%async_computation.8 | async-start | bytes 4718592 | tf_op jit(solution)/shard_map/reduce_scatter | solution.py:42
  204.4 274.9 %reduce-scatter.8.cloned.1.call-start = ((), (), s32[]{:S(2)}) async-start(), calls=%async_computation.9 | async-start | bytes 4718592 | tf_op jit(solution)/shard_map/reduce_scatter | solution.py:44
  204.7 6.1 %copy-start.4 = (bf16[2,1024,384]{1,2,0:T(8,128)(2,1)S(1)}, bf16[2,1024,384]{1,2,0:T(8,128)(2,1)}, u32[]{:S(2)}) copy-start(bf16[2,1024,384]{1,2,0:T(8,128)(2,1)} %copy-done.3) | copy-start | bytes 4718596
  204.7 6.1 %copy-start.9 = (bf16[2,2048,384]{2,1,0:T(8,128)(2,1)S(1)}, bf16[2,2048,384]{2,1,0:T(8,128)(2,1)}, u32[]{:S(2)}) copy-start(bf16[2,2048,384]{2,1,0:T(8,128)(2,1)} %param.12) | copy-start | bytes 9437188
Sparse Core Ops, SparseCore 0:
  10.1 127.1 all-gather.1
  178.9 34.9 reduce-scatter.11
  216.4 37.6 reduce-scatter.9
  257.1 37.7 reduce-scatter.13
  299.0 88.2 reduce-scatter.5
  391.3 87.9 reduce-scatter.7
